TPU v7x, 32 devices: a whole 2x2x4 slice. The times are simulated.
32 devices in a mesh: node: 4 (over y, x), feat: 4 (over z), tm: 2 (over core).
Axes of the slice: x: 2, y: 2, z: 4, core: 2. Of those that a mesh axis runs over, the one named last changes fastest.
Arguments:
- tensor: float32 [2, 16384, 4096], P('tm', 'node', 'feat'), may hold values from -6 to 6
- basis: float32 [16384, 128], P('node'), may hold values from -0.046875 to 0.046875
Outputs:
- gram: float32 [4096, 4096], P('feat', ('node', 'tm'))
All inputs are finite; a program needn't handle non-finite values.
Results may differ from a plain program's by a relative error of at most 0.000073.
Values sent between devices are 32-bit elements; how exact they have to be, the bound alone decides.
No kernel may reach another device: no remote copies, remote signals or barrier semaphores. Data moves between devices by JAX's collectives and lax.ppermute only.
A program may use at most 128 MiB of HBM per device.

v0:
```python
import jax
import jax.numpy as jnp
from jax import lax
from jax.sharding import PartitionSpec as P


def body(tensor, basis):
    local_data = tensor[0]
    partial_proj = lax.dot_general(
        basis,
        local_data,
        (((0,), (0,)), ((), ())),
        precision=lax.Precision.HIGHEST,
        preferred_element_type=jnp.float32,
    )
    scale = 1.0 / (basis.shape[1] * lax.axis_size("tm"))
    block_proj = lax.psum(partial_proj, "node")
    full_proj = lax.all_gather(block_proj, "feat", axis=1, tiled=True)
    width = full_proj.shape[1] // lax.axis_size("node")
    columns = lax.dynamic_slice_in_dim(full_proj, lax.axis_index("node") * width, width, 1)
    term = lax.dot_general(
        block_proj,
        columns,
        (((0,), (0,)), ((), ())),
        precision=lax.Precision.HIGHEST,
        preferred_element_type=jnp.float32,
    )
    result = lax.psum_scatter(term * scale, "tm", scatter_dimension=1, tiled=True)
    return result


def solution(mesh):
    in_specs = (P("tm", "node", "feat"), P("node", None))
    out_specs = P("feat", ("node", "tm"))
    return jax.shard_map(body, mesh=mesh, in_specs=in_specs, out_specs=out_specs, check_vma=False)
```

profile of v0, /device:TPU:0, one launch (start us, length us, event | category | flops | bytes accessed | tf_op | source)
XLA Modules:
  0.0 141.4 jit_solution(4735564744402768312)
XLA Ops:
  6.5 0.0 copy-start
  6.5 0.0 all-reduce.2.cloned.1.call-start
  6.5 1.6 %copy-done = f32[4096,128]{1,0:T(8,128)S(1)} copy-done((f32[4096,128]{1,0:T(8,128)S(1)}, f32[4096,128]{1,0:T(8,128)}, u32[]{:S(2)}) %copy-start) | copy-done | bytes 2097176
  8.1 13.5 %fusion = f32[128,1024]{1,0:T(8,128)} fusion(f32[4096,128]{1,0:T(8,128)S(1)} %copy-done, f32[1,4096,1024]{2,1,0:T(8,128)} %param.2), kind=kOutput, calls=%fused_computation | convolution fusion | flops 6442450944 | bytes 19398656 | tf_op jit(solution)/shard_map/dot_general | solution.py:9
  21.6 0.0 all-reduce.2.cloned.1.call-update
  21.6 0.0 all-gather.2.cloned.1.call-start
  21.7 48.1 %all-reduce.2.cloned.1.call-done = f32[128,1024]{1,0:T(8,128)} async-done(((f32[128,1024]{1,0:T(8,128)}), f32[128,1024]{1,0:T(8,128)}) %all-reduce.2.cloned.1.call-update) | async-done | bytes 524304 | tf_op jit(solution)/shard_map/psum | solution.py:17
  69.8 0.0 all-gather.2.cloned.1.call-update
  69.8 0.0 reduce-scatter.2.cloned.1.call-start
  69.9 47.5 %all-gather.2.cloned.1.call-done = f32[128,4096]{1,0:T(8,128)} async-done(((f32[128,1024]{1,0:T(8,128)}), f32[128,4096]{1,0:T(8,128)}) %all-gather.2.cloned.1.call-update) | async-done | bytes 2097168 | tf_op jit(solution)/shard_map/all_gather | solution.py:18
  117.3 6.6 %convolution_multiply_fusion = f32[1024,1024]{1,0:T(8,128)} fusion(f32[128,1024]{1,0:T(8,128)} %all-reduce.2.cloned.1.call-done, f32[128,4096]{1,0:T(8,128)} %all-gather.2.cloned.1.call-done, s32[]{:T(128)S(6)} %select_n.3), kind=kOutput, calls=%fused_computation.2 | convolution fusion | flops 1611661312 | bytes 5242884 | tf_op jit(solution)/shard_map/dot_general | solution.py:21
  124.0 0.0 reduce-scatter.2.cloned.1.call-update
  124.0 10.9 %reduce-scatter.2.cloned.1.call-done = f32[1024,512]{1,0:T(8,128)} async-done(((f32[1024,1024]{1,0:T(8,128)}), f32[1024,512]{1,0:T(8,128)}) %reduce-scatter.2.cloned.1.call-update) | async-done | bytes 2097168 | tf_op jit(solution)/shard_map/reduce_scatter | solution.py:28
Async XLA Ops:
  6.5 1.6 %copy-start = (f32[4096,128]{1,0:T(8,128)S(1)}, f32[4096,128]{1,0:T(8,128)}, u32[]{:S(2)}) copy-start(f32[4096,128]{1,0:T(8,128)} %param.3) | copy-start | bytes 6291460
  6.5 63.3 %all-reduce.2.cloned.1.call-start = ((), (), s32[]{:S(2)}) async-start(), calls=%async_computation.1 | async-start | bytes 1048576 | tf_op jit(solution)/shard_map/psum | solution.py:17
  21.6 95.7 %all-gather.2.cloned.1.call-start = ((), (), s32[]{:S(2)}) async-start(), calls=%async_computation.2 | async-start | bytes 2621440 | tf_op jit(solution)/shard_map/all_gather | solution.py:18
  69.8 65.1 %reduce-scatter.2.cloned.1.call-start = ((), (), s32[]{:S(2)}) async-start(), calls=%async_computation.3 | async-start | bytes 6291456 | tf_op jit(solution)/shard_map/reduce_scatter | solution.py:28
Sparse Core Ops, SparseCore 0:
  21.7 48.0 all-reduce.1
  71.4 45.9 all-gather.1
  124.1 10.7 reduce-scatter.1
where the time goes:
time: 142 us; the launch traced here: 141 us
  waiting for transfers between devices  107 us (75%)
  matrix products  20.1 us (14%)
  between operations  13.1 us (9%)
  local copies, waits for them, and re-layouts  1.59 us (1%)
    psum x1, waiting for transfers between devices, body(): block_proj = lax.psum(partial_proj, 'node')  48.1 us
    all_gather x1, waiting for transfers between devices, body(): full_proj = lax.all_gather(block_proj, 'feat', axis=1, tiled=True)  47.5 us
    dot_general x1, matrix products, body(): lax.dot_general(basis, local_data, (((0,), (0,)), ((), ())), precision=la...  13.5 us
    reduce_scatter x1, waiting for transfers between devices, body(): lax.psum_scatter(term * scale, 'tm', scatter_dimension=1, tiled=True)  10.9 us
    dot_general x1, matrix products, body(): lax.dot_general(block_proj, columns, (((0,), (0,)), ((), ())), precision=...  6.61 us
  transfers between devices with their start and end apart: 3, of which 3 were waited for; matrix products, arithmetic and copies ran while one was open for 0% of the time, Pallas kernels for 0%

commit v1 on v0

--- a/solution.py
+++ b/solution.py
@@ -15,7 +15,12 @@
     )
     scale = 1.0 / (basis.shape[1] * lax.axis_size("tm"))
     block_proj = lax.psum(partial_proj, "node")
-    full_proj = lax.all_gather(block_proj, "feat", axis=1, tiled=True)
+    ring = [block_proj]
+    for hop in range(3):
+        ring.append(lax.ppermute(ring[-1], "feat", [(dev, (dev + 1) % 4) for dev in range(4)]))
+    full_proj = jnp.roll(
+        jnp.concatenate(ring[::-1], axis=1), (lax.axis_index("feat") + 1) * ring[0].shape[1], axis=1
+    )
     width = full_proj.shape[1] // lax.axis_size("node")
     columns = lax.dynamic_slice_in_dim(full_proj, lax.axis_index("node") * width, width, 1)
     term = lax.dot_general(

time: 142 us -> 141 us (level)
  waiting for transfers between devices: 107 us -> 99.8 us
  local copies, waits for them, and re-layouts: 1.59 us -> 7.09 us
  starting transfers between devices: 0.08 us -> 1.53 us
    all_gather x1 -> x0, waiting for transfers between devices: 47.5 us -> none  [body(): full_proj = lax.all_gather(block_proj, 'feat', axis=1, tiled=True)]
    ppermute x0 -> x3, waiting for transfers between devices: none -> 42.2 us  [body(): lax.ppermute(ring[-1], 'feat', [(dev, (dev + 1) % 4) for dev in range(4)])]
    unnamed x2 -> x11, local copies, waits for them, and re-layouts: 1.59 us -> 7.05 us
    reduce_scatter x1, waiting for transfers between devices: 10.9 us -> 9.4 us  [body(): lax.psum_scatter(term * scale, 'tm', scatter_dimension=1, tiled=True)]
    ppermute x0 -> x3, starting transfers between devices: none -> 1.49 us  [body(): lax.ppermute(ring[-1], 'feat', [(dev, (dev + 1) % 4) for dev in range(4)])]
  transfers between devices with their start and end apart: 3 -> 5, of which waited for: 3 -> 5; matrix products, arithmetic and copies ran while one was open for 0% -> 0% of each run, Pallas kernels for 0% -> 0%
where the time goes in v1:
time: 141 us
  waiting for transfers between devices  99.8 us (71%)
  matrix products  18.7 us (13%)
  between operations  13.5 us (10%)
  local copies, waits for them, and re-layouts  7.09 us (5%)
  starting transfers between devices  1.53 us (1%)
    psum x1, waiting for transfers between devices, body(): block_proj = lax.psum(partial_proj, 'node')  48.1 us
    ppermute x3, waiting for transfers between devices, body(): lax.ppermute(ring[-1], 'feat', [(dev, (dev + 1) % 4) for dev in range(4)])  42.2 us
    dot_general x1, matrix products, body(): lax.dot_general(basis, local_data, (((0,), (0,)), ((), ())), precision=la...  13.5 us
    reduce_scatter x1, waiting for transfers between devices, body(): lax.psum_scatter(term * scale, 'tm', scatter_dimension=1, tiled=True)  9.4 us
    unnamed x11, local copies, waits for them, and re-layouts  7.05 us
    dot_general x1, matrix products, body(): lax.dot_general(block_proj, columns, (((0,), (0,)), ((), ())), precision=...  5.24 us
  transfers between devices with their start and end apart: 5, of which 5 were waited for; matrix products, arithmetic and copies ran while one was open for 0% of the time, Pallas kernels for 0%

profile of v1, /device:TPU:0, one launch (start us, length us, event | category | flops | bytes accessed | tf_op | source)
XLA Modules:
  0.0 140.6 jit_solution(5207033099549631223)
XLA Ops:
  6.5 0.0 copy-start
  6.5 0.0 all-reduce.2.cloned.1.call-start
  6.5 1.6 %copy-done = f32[4096,128]{1,0:T(8,128)S(1)} copy-done((f32[4096,128]{1,0:T(8,128)S(1)}, f32[4096,128]{1,0:T(8,128)}, u32[]{:S(2)}) %copy-start) | copy-done | bytes 2097176
  8.1 13.5 %fusion = f32[128,1024]{1,0:T(8,128)} fusion(f32[4096,128]{1,0:T(8,128)S(1)} %copy-done, f32[1,4096,1024]{2,1,0:T(8,128)} %param.2), kind=kOutput, calls=%fused_computation | convolution fusion | flops 6442450944 | bytes 19398656 | tf_op jit(solution)/shard_map/dot_general | solution.py:9
  21.6 0.0 all-reduce.2.cloned.1.call-update
  21.6 0.0 reduce-scatter.2.cloned.1.call-start
  21.7 48.1 %all-reduce.2.cloned.1.call-done = f32[128,1024]{1,0:T(8,128)} async-done(((f32[128,1024]{1,0:T(8,128)}), f32[128,1024]{1,0:T(8,128)}) %all-reduce.2.cloned.1.call-update) | async-done | bytes 524304 | tf_op jit(solution)/shard_map/psum | solution.py:17
  69.8 0.0 copy-start.1
  69.8 1.5 %collective-permute-start = (f32[128,1024]{1,0:T(8,128)}, f32[128,1024]{1,0:T(8,128)S(1)}, u32[]{:S(2)}, u32[]{:S(2)}) collective-permute-start(f32[128,1024]{1,0:T(8,128)} %all-reduce.2.cloned.1.call-done), channel_id=1, source_target_pairs={{0,2},{2,4},{4,6},{6,0},{1,3},{3,5},{5,7},{7,1},{8,10},{10,12},{12... | collective-permute-start | bytes 1572872 | tf_op jit(solution)/shard_map/ppermute | solution.py:20
  71.3 14.0 %collective-permute-done = f32[128,1024]{1,0:T(8,128)S(1)} collective-permute-done((f32[128,1024]{1,0:T(8,128)}, f32[128,1024]{1,0:T(8,128)S(1)}, u32[]{:S(2)}, u32[]{:S(2)}) %collective-permute-start) | collective-permute-done | bytes 524320 | tf_op jit(solution)/shard_map/ppermute | solution.py:20
  85.3 0.0 collective-permute-start.1
  85.3 14.5 %collective-permute-done.1 = f32[128,1024]{1,0:T(8,128)} collective-permute-done((f32[128,1024]{1,0:T(8,128)S(1)}, f32[128,1024]{1,0:T(8,128)}, u32[]{:S(2)}, u32[]{:S(2)}) %collective-permute-start.1) | collective-permute-done | bytes 524320 | tf_op jit(solution)/shard_map/ppermute | solution.py:20
  99.8 0.0 collective-permute-start.2
  99.8 13.8 %collective-permute-done.2 = f32[128,1024]{1,0:T(8,128)} collective-permute-done((f32[128,1024]{1,0:T(8,128)}, f32[128,1024]{1,0:T(8,128)}, u32[]{:S(2)}, u32[]{:S(2)}) %collective-permute-start.2) | collective-permute-done | bytes 524320 | tf_op jit(solution)/shard_map/ppermute | solution.py:20
  113.6 1.1 constant_dynamic-update-slice_fusion.7
  114.6 1.1 constant_dynamic-update-slice_fusion.6
  115.8 1.1 constant_dynamic-update-slice_fusion.4
  116.9 1.1 constant_dynamic-update-slice_fusion.3
  117.9 1.1 constant_dynamic-update-slice_fusion.2
  119.1 0.0 copy-done.1
  119.1 5.2 %convolution_multiply_fusion = f32[1024,1024]{1,0:T(8,128)} fusion(f32[128,1024]{1,0:T(8,128)S(1)} %copy-done.1, f32[128,8192]{1,0:T(8,128)S(1)} %constant_dynamic-update-slice_fusion, s32[]{:T(128)S(6)} %dynamic_slice.8), kind=kOutput, calls=%fused_computation.2 | convolution fusion | flops 1611661312 | bytes 5242884 | tf_op jit(solution)/shard_map/dot_general | solution.py:26
  124.4 0.0 reduce-scatter.2.cloned.1.call-update
  124.4 9.4 %reduce-scatter.2.cloned.1.call-done = f32[1024,512]{1,0:T(8,128)} async-done(((f32[1024,1024]{1,0:T(8,128)}), f32[1024,512]{1,0:T(8,128)}) %reduce-scatter.2.cloned.1.call-update) | async-done | bytes 2097168 | tf_op jit(solution)/shard_map/reduce_scatter | solution.py:33
  (3 shorter events, 0.1 us)
Async XLA Ops:
  6.5 1.6 %copy-start = (f32[4096,128]{1,0:T(8,128)S(1)}, f32[4096,128]{1,0:T(8,128)}, u32[]{:S(2)}) copy-start(f32[4096,128]{1,0:T(8,128)} %param.3) | copy-start | bytes 6291460
  6.5 63.3 %all-reduce.2.cloned.1.call-start = ((), (), s32[]{:S(2)}) async-start(), calls=%async_computation.1 | async-start | bytes 1048576 | tf_op jit(solution)/shard_map/psum | solution.py:17
  21.6 112.2 %reduce-scatter.2.cloned.1.call-start = ((), (), s32[]{:S(2)}) async-start(), calls=%async_computation.2 | async-start | bytes 6291456 | tf_op jit(solution)/shard_map/reduce_scatter | solution.py:33
  69.8 49.3 %copy-start.1 = (f32[128,1024]{1,0:T(8,128)S(1)}, f32[128,1024]{1,0:T(8,128)}, u32[]{:S(2)}) copy-start(f32[128,1024]{1,0:T(8,128)} %all-reduce.2.cloned.1.call-done) | copy-start | bytes 1572868
  69.8 15.5 %collective-permute-start = (f32[128,1024]{1,0:T(8,128)}, f32[128,1024]{1,0:T(8,128)S(1)}, u32[]{:S(2)}, u32[]{:S(2)}) collective-permute-start(f32[128,1024]{1,0:T(8,128)} %all-reduce.2.cloned.1.call-done), channel_id=1, source_target_pairs={{0,2},{2,4},{4,6},{6,0},{1,3},{3,5},{5,7},{7,1},{8,10},{10,12},{12... | collective-permute-start | bytes 1572872 | tf_op jit(solution)/shard_map/ppermute | solution.py:20
  85.3 14.5 %collective-permute-start.1 = (f32[128,1024]{1,0:T(8,128)S(1)}, f32[128,1024]{1,0:T(8,128)}, u32[]{:S(2)}, u32[]{:S(2)}) collective-permute-start(f32[128,1024]{1,0:T(8,128)S(1)} %collective-permute-done), channel_id=1, source_target_pairs={{0,2},{2,4},{4,6},{6,0},{1,3},{3,5},{5,7},{7,1},{8,10},{10,12},{12... | collective-permute-start | bytes 1572872 | tf_op jit(solution)/shard_map/ppermute | solution.py:20
  99.8 13.8 %collective-permute-start.2 = (f32[128,1024]{1,0:T(8,128)}, f32[128,1024]{1,0:T(8,128)}, u32[]{:S(2)}, u32[]{:S(2)}) collective-permute-start(f32[128,1024]{1,0:T(8,128)} %collective-permute-done.1), channel_id=1, source_target_pairs={{0,2},{2,4},{4,6},{6,0},{1,3},{3,5},{5,7},{7,1},{8,10},{10,12},{12... | collective-permute-start | bytes 1572872 | tf_op jit(solution)/shard_map/ppermute | solution.py:20
Sparse Core Ops, SparseCore 0:
  21.7 48.0 all-reduce.1
  124.5 9.2 reduce-scatter.1

commit v2 on v0

--- a/solution.py
+++ b/solution.py
@@ -14,7 +14,7 @@
         preferred_element_type=jnp.float32,
     )
     scale = 1.0 / (basis.shape[1] * lax.axis_size("tm"))
-    block_proj = lax.psum(partial_proj, "node")
+    block_proj = jnp.sum(lax.all_gather(partial_proj, "node"), axis=0)
     full_proj = lax.all_gather(block_proj, "feat", axis=1, tiled=True)
     width = full_proj.shape[1] // lax.axis_size("node")
     columns = lax.dynamic_slice_in_dim(full_proj, lax.axis_index("node") * width, width, 1)

time: 142 us -> 133 us (0.937)
  waiting for transfers between devices: 107 us -> 95.1 us
  other arithmetic: 0 us -> 2.59 us
    psum x1 -> x0, waiting for transfers between devices: 48.1 us -> none  [body(): block_proj = lax.psum(partial_proj, 'node')]
    all_gather x0 -> x1, waiting for transfers between devices: none -> 38.1 us  [body(): block_proj = jnp.sum(lax.all_gather(partial_proj, 'node'), axis=0)]
    reduce_sum x0 -> x1, other arithmetic: none -> 2.59 us  [body(): block_proj = jnp.sum(lax.all_gather(partial_proj, 'node'), axis=0)]
    all_gather x1, waiting for transfers between devices: 47.5 us -> 46 us  [body(): full_proj = lax.all_gather(block_proj, 'feat', axis=1, tiled=True)]
where the time goes in v2:
time: 133 us
  waiting for transfers between devices  95.1 us (72%)
  matrix products  20.1 us (15%)
  between operations  13.1 us (10%)
  other arithmetic  2.59 us (2%)
  local copies, waits for them, and re-layouts  1.59 us (1%)
    all_gather x1, waiting for transfers between devices, body(): full_proj = lax.all_gather(block_proj, 'feat', axis=1, tiled=True)  46 us
    all_gather x1, waiting for transfers between devices, body(): block_proj = jnp.sum(lax.all_gather(partial_proj, 'node'), axis=0)  38.1 us
    dot_general x1, matrix products, body(): lax.dot_general(basis, local_data, (((0,), (0,)), ((), ())), precision=la...  13.5 us
    reduce_scatter x1, waiting for transfers between devices, body(): lax.psum_scatter(term * scale, 'tm', scatter_dimension=1, tiled=True)  10.9 us
    dot_general x1, matrix products, body(): lax.dot_general(block_proj, columns, (((0,), (0,)), ((), ())), precision=...  6.61 us
  transfers between devices with their start and end apart: 3, of which 3 were waited for; matrix products, arithmetic and copies ran while one was open for 0% of the time, Pallas kernels for 0%

profile of v2, /device:TPU:0, one launch (start us, length us, event | category | flops | bytes accessed | tf_op | source)
XLA Modules:
  0.0 132.6 jit_solution(9680432985759834078)
XLA Ops:
  6.5 0.0 copy-start
  6.5 0.0 all-gather.6.cloned.1.call-start
  6.5 1.6 %copy-done = f32[4096,128]{1,0:T(8,128)S(1)} copy-done((f32[4096,128]{1,0:T(8,128)S(1)}, f32[4096,128]{1,0:T(8,128)}, u32[]{:S(2)}) %copy-start) | copy-done | bytes 2097176
  8.1 13.5 %fusion = f32[128,1024]{1,0:T(8,128)} fusion(f32[4096,128]{1,0:T(8,128)S(1)} %copy-done, f32[1,4096,1024]{2,1,0:T(8,128)} %param.2), kind=kOutput, calls=%fused_computation | convolution fusion | flops 6442450944 | bytes 19398656 | tf_op jit(solution)/shard_map/dot_general | solution.py:9
  21.6 0.0 all-gather.6.cloned.1.call-update
  21.6 0.0 all-gather.4.cloned.1.call-start
  21.7 38.1 %all-gather.6.cloned.1.call-done = f32[512,1024]{1,0:T(8,128)} async-done(((f32[128,1024]{1,0:T(8,128)}), f32[512,1024]{1,0:T(8,128)}) %all-gather.6.cloned.1.call-update) | async-done | bytes 2097168 | tf_op jit(solution)/shard_map/all_gather | solution.py:17
  59.8 2.6 %reduce_sum.9 = f32[128,1024]{1,0:T(8,128)} reduce(f32[4,128,1024]{2,1,0:T(8,128)} %bitcast.6, f32[]{:T(128)} %constant.6.clone.1), dimensions={0}, to_apply=%region_0.0 | reduce | flops 393216 | bytes 2621444 | tf_op jit(solution)/shard_map/reduce_sum | solution.py:17
  62.4 0.0 all-gather.4.cloned.1.call-update
  62.4 0.0 reduce-scatter.2.cloned.1.call-start
  62.5 46.0 %all-gather.4.cloned.1.call-done = f32[128,4096]{1,0:T(8,128)} async-done(((f32[128,1024]{1,0:T(8,128)}), f32[128,4096]{1,0:T(8,128)}) %all-gather.4.cloned.1.call-update) | async-done | bytes 2097168 | tf_op jit(solution)/shard_map/all_gather | solution.py:18
  108.5 6.6 %convolution_multiply_fusion = f32[1024,1024]{1,0:T(8,128)} fusion(f32[128,1024]{1,0:T(8,128)} %reduce_sum.9, f32[128,4096]{1,0:T(8,128)} %all-gather.4.cloned.1.call-done, s32[]{:T(128)S(6)} %select_n.3), kind=kOutput, calls=%fused_computation.2 | convolution fusion | flops 1611661312 | bytes 5242884 | tf_op jit(solution)/shard_map/dot_general | solution.py:21
  115.1 0.0 reduce-scatter.2.cloned.1.call-update
  115.1 10.9 %reduce-scatter.2.cloned.1.call-done = f32[1024,512]{1,0:T(8,128)} async-done(((f32[1024,1024]{1,0:T(8,128)}), f32[1024,512]{1,0:T(8,128)}) %reduce-scatter.2.cloned.1.call-update) | async-done | bytes 2097168 | tf_op jit(solution)/shard_map/reduce_scatter | solution.py:28
Async XLA Ops:
  6.5 1.6 %copy-start = (f32[4096,128]{1,0:T(8,128)S(1)}, f32[4096,128]{1,0:T(8,128)}, u32[]{:S(2)}) copy-start(f32[4096,128]{1,0:T(8,128)} %param.3) | copy-start | bytes 6291460
  6.5 53.2 %all-gather.6.cloned.1.call-start = ((), (), s32[]{:S(2)}) async-start(), calls=%async_computation.3 | async-start | bytes 2621440 | tf_op jit(solution)/shard_map/all_gather | solution.py:17
  21.6 86.9 %all-gather.4.cloned.1.call-start = ((), (), s32[]{:S(2)}) async-start(), calls=%async_computation.1 | async-start | bytes 2621440 | tf_op jit(solution)/shard_map/all_gather | solution.py:18
  62.4 63.6 %reduce-scatter.2.cloned.1.call-start = ((), (), s32[]{:S(2)}) async-start(), calls=%async_computation.2 | async-start | bytes 6291456 | tf_op jit(solution)/shard_map/reduce_scatter | solution.py:28
Sparse Core Ops, SparseCore 0:
  21.7 38.0 all-gather.5
  62.5 45.9 all-gather.3
  115.2 10.7 reduce-scatter.1
